TPU v7x, 256 devices: a whole 4x4x8 slice. The times are simulated.
256 devices in a mesh: blk: 16 (over z, x_hi), leaf: 8 (over y, core), rhs: 2 (over x_lo).
Axes of the slice: x: 4 (x_hi: 2, x_lo: 2; x = x_hi * 2 + x_lo), y: 4, z: 8, core: 2. Of those that a mesh axis runs over, the one named last changes fastest.
Arguments:
- residual: float32 [32, 8, 65536], P('rhs', 'leaf', 'blk'), may hold values from -160 to 160
- points: float32 [3, 8, 65536], P(None, 'leaf', 'blk'), may hold values from -12330 to 12330
- noise: float32 [8, 65536], P('leaf', 'blk'), may hold values from 1 to 2
- block_list: int32 [8, 8, 256], P('leaf'), may hold values from 0 to 1, as said below
Outputs:
- correction: float32 [32, 8, 65536], P('rhs', 'leaf', 'blk')
- new_residual: float32 [32, 8, 65536], P('rhs', 'leaf', 'blk')
- basis: float32 [128, 8, 65536], P('rhs', 'leaf', 'blk')
Inputs may be any that keep to these rules, and one draw needn't show every extreme that they name: The list is symmetric: block_list[t, k, i] == block_list[t, 7 - k, (i + d) mod 256] with d the offset of entry k.
All inputs are finite; a program needn't handle non-finite values.
Results may differ from a plain program's by a relative error of at most 0.007.
Values sent between devices are 32-bit elements; how exact they have to be, the bound alone decides.
A program may use at most 128 MiB of HBM per device.

v0:
```python
import jax
import jax.numpy as jnp
from jax import lax
from jax.sharding import PartitionSpec as P

M = 32
S = 4
BS = 256
REACH = 4
SUPPORT = 1408
centre_shift = 1.5
amplitude = 1.1
exact = lax.Precision.HIGHEST


def extended(x, sides, width):
    for axis, dim in sides:
        count, length = (lax.axis_size(axis), x.shape[dim])
        up = [(i, (i + 1) % count) for i in range(count)]
        down = [(j, i) for i, j in up]
        last = lax.slice_in_dim(x, length - width, length, axis=dim)
        leading = lax.slice_in_dim(x, 0, width, axis=dim)
        before = lax.ppermute(last, axis, up)
        after = lax.ppermute(leading, axis, down)
        x = jnp.concatenate([before, x, after], axis=dim)
    return x


def kernel_tile(near_points, own_points):
    squared = (near_points[0][:, None] - own_points[0][None, :]) ** 2
    squared = squared + (near_points[1][:, None] - own_points[1][None, :]) ** 2
    squared = squared + (near_points[2][:, None] - own_points[2][None, :]) ** 2
    radius = jnp.sqrt(squared) / SUPPORT
    remain = jnp.maximum(1.0 - radius, 0.0)
    return remain * remain * (remain * remain) * (4.0 * radius + 1.0) * (amplitude / SUPPORT)


def band_product(field_wide, points_wide, weights, rows_out):
    per_turn = rows_out // 8
    count = field_wide.shape[0]

    def turn(carry, index):
        pieces = []
        for inner in range(per_turn):
            block = index * per_turn + inner
            own_points = lax.dynamic_slice_in_dim(points_wide, (block + REACH) * BS, BS, 1)
            total = jnp.zeros((count, BS), jnp.float32)
            for offset in range(2 * REACH + 1):
                column_at = (block + offset) * BS
                near_points = lax.dynamic_slice_in_dim(points_wide, column_at, BS, 1)
                near_field = lax.dynamic_slice_in_dim(field_wide, column_at, BS, 1)
                listed = lax.dynamic_index_in_dim(weights[offset], block, 0, False)
                tile = kernel_tile(near_points, own_points) * listed
                total = total + jnp.dot(near_field, tile, precision=exact)
            pieces.append(total)
        return (carry, jnp.concatenate(pieces, axis=1))

    carry, parts = lax.scan(turn, jnp.zeros((), jnp.int32), jnp.arange(8, dtype=jnp.int32))
    return jnp.moveaxis(parts, 0, 1).reshape(count, rows_out * BS)


def galerkin(gram, count_points, count_sides):
    normed = gram / count_points
    basis_count = normed.shape[0]
    gram_basis = normed[:basis_count, :basis_count]
    factor_low = jnp.linalg.cholesky(gram_basis)
    inverse_low = lax.linalg.triangular_solve(
        factor_low, jnp.eye(basis_count, dtype=jnp.float32), left_side=True, lower=True
    )
    cross = normed[:basis_count, count_sides:] + centre_shift * gram_basis
    projected = jnp.dot(
        jnp.dot(inverse_low, cross, precision=exact), inverse_low.T, precision=exact
    )
    projected = 0.5 * (projected + projected.T)
    small_side = jnp.dot(inverse_low, gram_basis[:, :count_sides], precision=exact)
    proj_factor = jnp.linalg.cholesky(projected)
    halfway = lax.linalg.triangular_solve(proj_factor, small_side, left_side=True, lower=True)
    coeffs = lax.linalg.triangular_solve(
        proj_factor, halfway, left_side=True, lower=True, transpose_a=True
    )
    combo = jnp.dot(coeffs.T, inverse_low, precision=exact)
    return (inverse_low, combo)


def row_products(rows, cols):
    return lax.dot_general(rows, cols, (((1,), (1,)), ((), ())), precision=exact)


def butterfly_sum(x, axes):
    for axis in axes:
        count = lax.axis_size(axis)
        if count & count - 1:
            x = lax.psum(x, axis)
            continue
        step = 1
        while step < count:
            x = x + lax.ppermute(x, axis, [(i, i ^ step) for i in range(count)])
            step *= 2
    return x


def local(residual, points, noise, block_list):
    field = residual[:, 0]
    coords = points[:, 0]
    nugget = noise[0]
    own_rows = field.shape[1]
    own_blocks = own_rows // BS
    first_block = lax.axis_index("blk") * own_blocks
    listed = block_list[0].astype(jnp.float32)
    nine = jnp.concatenate(
        [listed[:REACH], jnp.ones((1, listed.shape[1]), jnp.float32), listed[REACH:]], axis=0
    )
    margin = S * REACH
    wrapped = jnp.concatenate([nine[:, -margin:], nine, nine[:, :margin]], axis=1)
    powers = [field]
    rim = REACH * BS
    coords_wide = extended(coords, (("blk", 1),), rim)
    own_weights = lax.dynamic_slice_in_dim(wrapped, first_block + margin, own_blocks, 1)
    current = field
    for power_step in range(S):
        widened = extended(current, (("blk", 1),), rim)
        current = (
            band_product(widened, coords_wide, own_weights, own_blocks)
            + (nugget - centre_shift) * current
        )
        powers.append(current)
    half_panel = jnp.stack(powers, axis=0)
    count_points = own_rows * lax.axis_size("blk") * lax.axis_size("leaf")
    sides_here = field.shape[0]
    whole = lax.all_gather(half_panel, "rhs", axis=1, tiled=True)
    flat = whole.reshape(-1, own_rows)
    gram = butterfly_sum(row_products(flat[: S * M], flat), ("leaf", "blk"))
    inverse_low, combo = galerkin(gram, count_points, M)
    first_rows = flat[: S * M]
    image = flat[M:] + centre_shift * first_rows
    part = lax.axis_index("rhs")
    basis_here = S * M // lax.axis_size("rhs")
    mine_low = lax.dynamic_slice_in_dim(inverse_low, part * basis_here, basis_here, 0)
    mine_combo = lax.dynamic_slice_in_dim(combo, part * sides_here, sides_here, 0)
    correction = jnp.dot(mine_combo, first_rows, precision=exact)
    new_residual = field - jnp.dot(mine_combo, image, precision=exact)
    basis = jnp.dot(mine_low, first_rows, precision=exact)
    return (correction[:, None], new_residual[:, None], basis[:, None])


def solution(mesh):
    placed = (
        P("rhs", "leaf", "blk"),
        P(None, "leaf", "blk"),
        P("leaf", "blk"),
        P("leaf", None, None),
    )
    return jax.shard_map(
        local,
        mesh=mesh,
        in_specs=placed,
        out_specs=(P("rhs", "leaf", "blk"), P("rhs", "leaf", "blk"), P("rhs", "leaf", "blk")),
        check_vma=False,
    )
```

profile of v0, /device:TPU:8, one launch (start us, length us, event | category | flops | bytes accessed | tf_op | source)
XLA Modules:
  0.0 1043.5 jit_solution(11603520780824057718)
XLA Ops:
  7.2 1.1 copy.44
  8.3 8.4 collective-permute-start.1
  16.7 0.8 copy.45
  17.6 5.7 collective-permute-start.3
  23.3 1.1 bitcast_dynamic-update-slice_fusion
  24.4 0.7 convert_element_type.5
  25.2 0.7 broadcast_add_fusion
  26.0 4.6 collective-permute-done.2
  30.8 209.0 %while.52 = (s32[]{:T(128)}, f32[8,16,512]{2,1,0:T(8,128)S(1)}, s32[8]{0:T(128)S(1)}, f32[16,6144]{1,0:T(8,128)S(1)}, f32[3,6144]{1,0:T(4,128)S(1)}, /*index=5*/...) while((s32[]{:T(128)}, f32[8,16,512]{2,1,0:T(8,128)S(1)}, ...), condition=%wide.region_1.2_spmd, body=%wide.region_0.1_spmd.sunk | while | flops 246620224 | bytes 1092197 | solution.py:58
  43.6 0.7 constant_dynamic-slice_fusion.141
  69.8 0.7 constant_dynamic-slice_fusion.141
  95.9 0.7 constant_dynamic-slice_fusion.141
  122.0 0.7 constant_dynamic-slice_fusion.141
  148.1 0.7 constant_dynamic-slice_fusion.141
  174.3 0.7 constant_dynamic-slice_fusion.141
  200.4 0.7 constant_dynamic-slice_fusion.141
  226.5 0.7 constant_dynamic-slice_fusion.141
  240.3 1.3 collective-permute-start.5
  241.6 2.5 collective-permute-start.4
  244.3 2.1 collective-permute-done.5
  246.3 3.1 collective-permute-done.4
  249.6 208.9 %while.53 = (s32[]{:T(128)}, f32[8,16,512]{2,1,0:T(8,128)S(1)}, s32[8]{0:T(128)S(1)}, f32[16,6144]{1,0:T(8,128)S(1)}, f32[3,6144]{1,0:T(4,128)S(1)}, /*index=5*/...) while((s32[]{:T(128)}, f32[8,16,512]{2,1,0:T(8,128)S(1)}, ...), condition=%wide.region_3.4_spmd, body=%wide.region_2.3_spmd.sunk | while | flops 246620224 | bytes 1092197 | solution.py:58
  262.3 0.7 constant_dynamic-slice_fusion.147
  288.4 0.7 constant_dynamic-slice_fusion.147
  314.5 0.7 constant_dynamic-slice_fusion.147
  340.6 0.7 constant_dynamic-slice_fusion.147
  366.7 0.7 constant_dynamic-slice_fusion.147
  392.8 0.7 constant_dynamic-slice_fusion.147
  418.9 0.7 constant_dynamic-slice_fusion.147
  445.1 0.7 constant_dynamic-slice_fusion.147
  458.9 3.9 collective-permute-start.6
  462.8 1.8 collective-permute-done.7
  464.6 2.6 collective-permute-done.6
  467.3 208.6 %while.54 = (s32[]{:T(128)}, f32[8,16,512]{2,1,0:T(8,128)S(1)}, s32[8]{0:T(128)S(1)}, f32[16,6144]{1,0:T(8,128)S(1)}, f32[3,6144]{1,0:T(4,128)S(1)}, /*index=5*/...) while((s32[]{:T(128)}, f32[8,16,512]{2,1,0:T(8,128)S(1)}, ...), condition=%wide.region_5.6_spmd, body=%wide.region_4.5_spmd.sunk | while | flops 246620224 | bytes 1092197 | solution.py:58
  676.3 3.7 collective-permute-start.8
  680.1 2.0 collective-permute-done.9
  682.1 2.4 collective-permute-done.8
  684.5 209.2 %while.55 = (s32[]{:T(128)}, f32[8,16,512]{2,1,0:T(8,128)S(1)}, s32[8]{0:T(128)S(1)}, f32[16,6144]{1,0:T(8,128)S(1)}, f32[3,6144]{1,0:T(4,128)S(1)}, /*index=5*/...) while((s32[]{:T(128)}, f32[8,16,512]{2,1,0:T(8,128)S(1)}, ...), condition=%wide.region_7.8_spmd, body=%wide.region_6.7_spmd.sunk | while | flops 246620224 | bytes 1092197 | solution.py:58
  894.1 1.1 copy-done.3
  895.1 39.7 %all-gather.2.cloned.1.call-done = f32[5,32,4096]{2,1,0:T(8,128)} async-done(((f32[5,16,4096]{2,1,0:T(8,128)}), f32[5,32,4096]{2,1,0:T(8,128)}) %all-gather.2.cloned.1.call-update) | async-done | bytes 2621456 | tf_op jit(solution)/shard_map/all_gather | solution.py:130
  934.8 4.1 fusion.2570
  938.9 2.2 fusion.2577
  941.2 1.3 collective-permute-done.10
  943.1 4.0 collective-permute-done.11
  947.1 2.2 collective-permute-start.12
  949.3 3.8 collective-permute-done.12
  953.2 3.0 collective-permute-start.13
  956.2 3.3 collective-permute-done.13
  959.4 1.6 collective-permute-start.14
  961.1 3.8 collective-permute-done.14
  964.9 2.0 collective-permute-start.15
  966.8 4.3 collective-permute-done.15
  971.2 6.3 collective-permute-start.16
  977.5 3.2 bitcast_add_fusion
  980.8 11.7 %cholesky.44 = f32[128,128]{1,0:T(8,128)S(1)} custom-call(f32[128,128]{1,0:T(8,128)S(1)} %fusion.2546), custom_call_target="Cholesky" | custom-call | tf_op jit(solution)/shard_map/jit(cholesky)/cholesky | solution.py:66
  993.9 9.8 custom-call.10
  1004.9 11.7 %cholesky.55 = f32[128,128]{1,0:T(8,128)S(1)} custom-call(f32[128,128]{1,0:T(8,128)S(1)} %fusion.2542), custom_call_target="Cholesky" | custom-call | tf_op jit(solution)/shard_map/jit(cholesky)/cholesky | solution.py:76
  1018.0 10.0 custom-call.11
  1028.8 1.1 convolution_bitcast_fusion.1
  1029.9 1.0 copy.26
  1030.9 1.1 fusion.2532
  1032.0 1.0 copy.27
  1033.0 1.2 convolution_bitcast_fusion
  1034.2 2.0 copy.28
  (935 shorter events, 402.8 us)
Async XLA Ops:
  7.2 927.7 %all-gather.2.cloned.1.call-start = ((), (), s32[]{:S(2)}) async-start(), calls=%async_computation | async-start | bytes 3932160 | tf_op jit(solution)/shard_map/all_gather | solution.py:130
  8.3 22.3 %collective-permute-start.1 = (f32[16,1024]{1,0:T(8,128)S(1)}, f32[16,1024]{1,0:T(8,128)S(1)}, u32[]{:S(2)}, u32[]{:S(2)}) collective-permute-start(f32[16,1024]{1,0:T(8,128)S(1)} %get-tuple-element.897), channel_id=1, source_target_pairs={{16,0},{32,16},{48,32},{64,48},{80,64},{96,80},{112,96},{128,112},... | collective-permute-start | bytes 196616 | tf_op jit(solution)/shard_map/ppermute | solution.py:24
  16.7 14.0 %collective-permute-start = (f32[16,1024]{1,0:T(8,128)S(1)}, f32[16,1024]{1,0:T(8,128)S(1)}, u32[]{:S(2)}, u32[]{:S(2)}) collective-permute-start(f32[16,1024]{1,0:T(8,128)S(1)} %get-tuple-element.896), channel_id=1, source_target_pairs={{0,16},{16,32},{32,48},{48,64},{64,80},{80,96},{96,112},{112,128},... | collective-permute-start | bytes 196616 | tf_op jit(solution)/shard_map/ppermute | solution.py:23
  17.6 8.5 collective-permute-start.3
  23.3 7.4 collective-permute-start.2
  30.8 209.3 %copy-start.2 = (f32[16,1,4096]{2,1,0:T(1,128)S(1)}, f32[16,1,4096]{2,1,0:T(1,128)}, u32[]{:S(2)}) copy-start(f32[16,1,4096]{2,1,0:T(1,128)} %param.13) | copy-start | bytes 786436
  240.3 6.1 collective-permute-start.5
  241.6 7.9 collective-permute-start.4
  458.8 5.8 collective-permute-start.7
  458.9 8.4 collective-permute-start.6
  676.2 5.8 collective-permute-start.9
  676.3 8.1 collective-permute-start.8
  894.1 1.1 copy-start.3
  934.8 4.1 copy-start
  941.1 1.4 collective-permute-start.10
  942.5 4.6 collective-permute-start.11
  947.1 6.0 collective-permute-start.12
  953.2 6.2 collective-permute-start.13
  959.4 5.4 collective-permute-start.14
  964.9 6.3 collective-permute-start.15
  971.2 9.5 collective-permute-start.16
  1028.0 2.8 copy-start.1
Sparse Core Ops, SparseCore 0:
  895.3 39.5 all-gather.1
where the time goes:
time: 1060 us; the launch traced here: 1040 us
  loops' own time  429 us (40%)
  matrix products  279 us (26%)
  local copies, waits for them, and re-layouts  147 us (14%)
  waiting for transfers between devices  78.7 us (7%)
  other arithmetic  52.4 us (5%)
  starting transfers between devices  41.6 us (4%)
  between operations  15 us (1%)
    another operation x4, loops' own time, band_product(): lax.scan(turn, jnp.zeros((), jnp.int32), jnp.arange(8, dtype=jnp.int32))  429 us
    dot_general x576, matrix products, turn(): total = total + jnp.dot(near_field, tile, precision=exact)  272 us
    dynamic_slice x160, local copies, waits for them, and re-layouts, turn(): listed = lax.dynamic_index_in_dim(weights[offset], block, 0, False)  109 us
    all_gather x1, waiting for transfers between devices, local(): whole = lax.all_gather(half_panel, 'rhs', axis=1, tiled=True)  39.7 us
  transfers between devices with their start and end apart: 18, of which 14 were waited for; matrix products, arithmetic and copies ran while one was open for 1% of the time, Pallas kernels for 0%

commit v1 on v0

--- a/solution.py
+++ b/solution.py
@@ -127,7 +127,9 @@
     half_panel = jnp.stack(powers, axis=0)
     count_points = own_rows * lax.axis_size("blk") * lax.axis_size("leaf")
     sides_here = field.shape[0]
-    whole = lax.all_gather(half_panel, "rhs", axis=1, tiled=True)
+    whole = jnp.concatenate(
+        lax.all_to_all(jnp.stack([half_panel] * lax.axis_size("rhs")), "rhs", 0, 0), axis=1
+    )
     flat = whole.reshape(-1, own_rows)
     gram = butterfly_sum(row_products(flat[: S * M], flat), ("leaf", "blk"))
     inverse_low, combo = galerkin(gram, count_points, M)

time: 1060 us -> 1020 us (0.962)
  waiting for transfers between devices: 78.7 us -> 27.4 us
  blocking collectives: 0 us -> 29.1 us
  between operations: 15 us -> 1.65 us
    all_gather x1 -> x0, waiting for transfers between devices: 39.7 us -> none  [local(): whole = lax.all_gather(half_panel, 'rhs', axis=1, tiled=True)]
    all_to_all x0 -> x1, blocking collectives: none -> 29.1 us  [local(): lax.all_to_all(jnp.stack([half_panel] * lax.axis_size('rhs')), 'rhs', 0, 0)]
    ppermute x5, starting transfers between devices: 15.6 us -> 28.6 us  [extended(): after = lax.ppermute(leading, axis, down)]
  transfers between devices with their start and end apart: 18 -> 17, of which waited for: 14 -> 11; matrix products, arithmetic and copies ran while one was open for 1% -> 1% of each run, Pallas kernels for 0% -> 0%
where the time goes in v1:
time: 1020 us; the launch traced here: 1010 us
  loops' own time  429 us (42%)
  matrix products  279 us (27%)
  local copies, waits for them, and re-layouts  144 us (14%)
  other arithmetic  51.1 us (5%)
  starting transfers between devices  45.3 us (4%)
  blocking collectives  29.1 us (3%)
  waiting for transfers between devices  27.4 us (3%)
    another operation x4, loops' own time, band_product(): lax.scan(turn, jnp.zeros((), jnp.int32), jnp.arange(8, dtype=jnp.int32))  429 us
    dot_general x576, matrix products, turn(): total = total + jnp.dot(near_field, tile, precision=exact)  272 us
    dynamic_slice x160, local copies, waits for them, and re-layouts, turn(): listed = lax.dynamic_index_in_dim(weights[offset], block, 0, False)  107 us
    all_to_all x1, blocking collectives, local(): lax.all_to_all(jnp.stack([half_panel] * lax.axis_size('rhs')), 'rhs', 0, 0)  29.1 us
    ppermute x5, starting transfers between devices, extended(): after = lax.ppermute(leading, axis, down)  28.6 us
    ppermute x7, waiting for transfers between devices, butterfly_sum(): x = x + lax.ppermute(x, axis, [(i, i ^ step) for i in range(count)])  22.5 us
  transfers between devices with their start and end apart: 17, of which 11 were waited for; matrix products, arithmetic and copies ran while one was open for 1% of the time, Pallas kernels for 0%

profile of v1, /device:TPU:8, one launch (start us, length us, event | category | flops | bytes accessed | tf_op | source)
XLA Modules:
  0.0 1006.6 jit_solution(8588473101267761764)
XLA Ops:
  0.6 0.8 copy.48
  1.5 3.1 collective-permute-start.2
  4.6 5.4 collective-permute-start.3
  10.0 1.1 copy.47
  11.2 5.6 collective-permute-start.1
  16.8 1.1 bitcast_dynamic-update-slice_fusion
  17.9 0.7 convert_element_type.5
  18.7 0.7 broadcast_add_fusion
  19.7 208.2 %while.52 = (s32[]{:T(128)}, f32[8,16,512]{2,1,0:T(8,128)S(1)}, s32[8]{0:T(128)S(1)}, f32[16,6144]{1,0:T(8,128)S(1)}, f32[3,6144]{1,0:T(4,128)S(1)}, /*index=5*/...) while((s32[]{:T(128)}, f32[8,16,512]{2,1,0:T(8,128)S(1)}, ...), condition=%wide.region_1.2_spmd, body=%wide.region_0.1_spmd.sunk | while | flops 246620224 | bytes 1092189 | solution.py:58
  32.4 0.7 constant_dynamic-slice_fusion.141
  84.5 0.7 constant_dynamic-slice_fusion.141
  110.5 0.7 constant_dynamic-slice_fusion.141
  136.5 0.7 constant_dynamic-slice_fusion.141
  162.5 0.7 constant_dynamic-slice_fusion.141
  188.6 0.7 constant_dynamic-slice_fusion.141
  214.6 0.7 constant_dynamic-slice_fusion.141
  228.2 5.9 collective-permute-start.5
  234.5 1.6 collective-permute-done.4
  236.1 208.9 %while.53 = (s32[]{:T(128)}, f32[8,16,512]{2,1,0:T(8,128)S(1)}, s32[8]{0:T(128)S(1)}, f32[16,6144]{1,0:T(8,128)S(1)}, f32[3,6144]{1,0:T(4,128)S(1)}, /*index=5*/...) while((s32[]{:T(128)}, f32[8,16,512]{2,1,0:T(8,128)S(1)}, ...), condition=%wide.region_3.4_spmd, body=%wide.region_2.3_spmd.sunk | while | flops 246620224 | bytes 1092189 | solution.py:58
  243.0 0.7 constant_dynamic-slice_fusion.145
  295.2 0.7 constant_dynamic-slice_fusion.145
  321.3 0.7 constant_dynamic-slice_fusion.145
  347.5 0.7 constant_dynamic-slice_fusion.145
  445.3 6.4 collective-permute-start.7
  451.9 1.5 collective-permute-done.6
  453.6 207.4 %while.54 = (s32[]{:T(128)}, f32[8,16,512]{2,1,0:T(8,128)S(1)}, s32[8]{0:T(128)S(1)}, f32[16,6144]{1,0:T(8,128)S(1)}, f32[3,6144]{1,0:T(4,128)S(1)}, /*index=5*/...) while((s32[]{:T(128)}, f32[8,16,512]{2,1,0:T(8,128)S(1)}, ...), condition=%wide.region_5.6_spmd, body=%wide.region_4.5_spmd.sunk | while | flops 246620224 | bytes 1092189 | solution.py:58
  661.1 0.9 collective-permute-start.8
  662.0 5.4 collective-permute-start.9
  667.7 1.7 collective-permute-done.8
  669.4 208.7 %while.55 = (s32[]{:T(128)}, f32[8,16,512]{2,1,0:T(8,128)S(1)}, s32[8]{0:T(128)S(1)}, f32[16,6144]{1,0:T(8,128)S(1)}, f32[3,6144]{1,0:T(4,128)S(1)}, /*index=5*/...) while((s32[]{:T(128)}, f32[8,16,512]{2,1,0:T(8,128)S(1)}, ...), condition=%wide.region_7.8_spmd, body=%wide.region_6.7_spmd.sunk | while | flops 246620224 | bytes 1092189 | solution.py:58
  673.3 0.7 constant_dynamic-slice_fusion.156
  699.4 0.7 constant_dynamic-slice_fusion.156
  725.5 0.7 constant_dynamic-slice_fusion.156
  751.6 0.7 constant_dynamic-slice_fusion.156
  777.7 0.7 constant_dynamic-slice_fusion.156
  803.7 0.7 constant_dynamic-slice_fusion.156
  829.8 0.7 constant_dynamic-slice_fusion.156
  855.9 0.7 constant_dynamic-slice_fusion.156
  878.7 29.1 %all_to_all.5 = f32[2,5,16,4096]{3,2,1,0:T(8,128)S(1)} all-to-all(f32[2,5,16,4096]{3,2,1,0:T(8,128)S(1)} %pad_maximum_fusion), channel_id=1, replica_groups=mesh['blk'=16,'leaf'=8,'rhs'=2] {'rhs'}, dimensions={0} | all-to-all | bytes 5242880 | tf_op jit(solution)/shard_map/all_to_all | solution.py:131
  907.8 1.8 fusion.2570
  910.0 2.2 fusion.2577
  912.3 1.3 collective-permute-done.10
  914.1 4.1 collective-permute-done.11
  918.2 2.4 collective-permute-start.12
  920.6 3.6 collective-permute-done.12
  924.3 5.9 collective-permute-done.13
  930.3 1.4 collective-permute-start.14
  931.6 3.2 collective-permute-done.14
  934.8 4.4 collective-permute-start.15
  939.2 1.7 copy.28
  941.0 1.0 collective-permute-done.15
  942.0 3.6 collective-permute-start.16
  945.5 1.6 bitcast_add_fusion
  947.1 3.5 collective-permute-done.16
  950.7 11.7 %cholesky.44 = f32[128,128]{1,0:T(8,128)S(1)} custom-call(f32[128,128]{1,0:T(8,128)S(1)} %fusion.2546), custom_call_target="Cholesky" | custom-call | tf_op jit(solution)/shard_map/jit(cholesky)/cholesky | solution.py:66
  963.8 9.8 custom-call.10
  974.3 1.2 convolution_bitcast_fusion
  975.6 2.0 copy.31
  978.1 12.0 %cholesky.55 = f32[128,128]{1,0:T(8,128)S(1)} custom-call(f32[128,128]{1,0:T(8,128)S(1)} %fusion.2542), custom_call_target="Cholesky" | custom-call | tf_op jit(solution)/shard_map/jit(cholesky)/cholesky | solution.py:76
  991.4 9.8 custom-call.11
  1002.0 1.1 convolution_bitcast_fusion.1
  1003.1 1.1 fusion.2532
  1004.2 1.0 copy.30
  1005.2 1.0 copy.29
  (933 shorter events, 399.6 us)
Async XLA Ops:
  1.5 18.1 %collective-permute-start.2 = (f32[3,1024]{1,0:T(4,128)S(1)}, f32[3,1024]{1,0:T(4,128)S(1)}, u32[]{:S(2)}, u32[]{:S(2)}) collective-permute-start(f32[3,1024]{1,0:T(4,128)S(1)} %get-tuple-element.898), channel_id=1, source_target_pairs={{0,16},{16,32},{32,48},{48,64},{64,80},{80,96},{96,112},{112,128},... | collective-permute-start | bytes 36872 | tf_op jit(solution)/shard_map/ppermute | solution.py:23
  4.6 15.0 %collective-permute-start.3 = (f32[3,1024]{1,0:T(4,128)S(1)}, f32[3,1024]{1,0:T(4,128)S(1)}, u32[]{:S(2)}, u32[]{:S(2)}) collective-permute-start(f32[3,1024]{1,0:T(4,128)S(1)} %get-tuple-element.899), channel_id=1, source_target_pairs={{16,0},{32,16},{48,32},{64,48},{80,64},{96,80},{112,96},{128,112},... | collective-permute-start | bytes 36872 | tf_op jit(solution)/shard_map/ppermute | solution.py:24
  11.1 8.5 collective-permute-start
  11.2 8.4 collective-permute-start.1
  19.7 208.2 %copy-start.1 = (f32[16,1,4096]{2,1,0:T(1,128)S(1)}, f32[16,1,4096]{2,1,0:T(1,128)}, u32[]{:S(2)}) copy-start(f32[16,1,4096]{2,1,0:T(1,128)} %param.13) | copy-start | bytes 786436
  228.1 8.0 collective-permute-start.4
  228.2 7.9 collective-permute-start.5
  445.2 8.2 collective-permute-start.6
  445.3 8.3 collective-permute-start.7
  661.1 8.3 collective-permute-start.8
  662.0 7.4 collective-permute-start.9
  912.2 1.4 collective-permute-start.10
  913.6 4.6 collective-permute-start.11
  918.2 6.0 collective-permute-start.12
  924.2 6.0 collective-permute-start.13
  930.3 4.5 collective-permute-start.14
  934.8 7.1 collective-permute-start.15
  942.0 8.6 collective-permute-start.16
  1001.2 1.9 copy-start
